TPU v7x, 512 devices: a whole 4x8x8 slice. The times are simulated.
512 devices in a mesh: layer: 16 (over z, core), plane: 32 (over x, y).
Axes of the slice: x: 4, y: 8, z: 8, core: 2. Of those that a mesh axis runs over, the one named last changes fastest.
Arguments:
- velocity: bfloat16 [2, 128, 131072], P(None, 'layer', 'plane'), may hold values from -6 to 6
- adjoint: bfloat16 [2, 128, 131072], P(None, 'layer', 'plane'), may hold values from -6 to 6
- corners: int32 [4, 131072], P(None, 'plane'), may hold values from 0 to 4607, as said below
- shared: int32 [4, 4096], P(None, 'plane'), may hold values from 0 to 4096, as said below
- stretch: float32 [2, 131072], P(None, 'plane'), may hold values from 0.5 to 2
- shear_part: float32 [2, 131072], P(None, 'plane'), may hold values from -0.2 to 0.2
- thickness: float32 [128, 131072], P('layer', 'plane'), may hold values from 0.3 to 3
- rate_factor: float32 [128, 131072], P('layer', 'plane'), may hold values from 0.5 to 2
- retention: float32 [128, 131072], P('layer', 'plane'), may hold values from 0.2 to 1
- weight: float32 [128, 131072], P('layer', 'plane'), may hold values from 0.5 to 2
Outputs:
- gradient: float32 [131072], P('plane')
Inputs may be any that keep to these rules, and one draw needn't show every extreme that they name: `corners`: below 4096 a number names an owned node; 4096 + j * 128 + s names slot s of the ghost block of direction j (plane offsets -2, -1, +1, +2). Every slot of a block whose partition exists is named by exactly one corner, corner 0 of some element; blocks of directions beyond the ends of the plane axis are named by none. `shared`: row j, block p lists 128 distinct owned nodes of partition p that the partition at offset o_j (-2, -1, +1, +2) holds as ghosts; the block is 4096 throughout where that partition does not exist.
All inputs are finite; a program needn't handle non-finite values.
Results may differ from a plain program's by a relative error of at most 0.0003.
Values may be sent and summed in bfloat16 or wider, within the bound.
A program may use at most 128 MiB of HBM per device.

v0:
```python
import math
import jax
import jax.numpy as jnp
from jax import lax
from jax.sharding import PartitionSpec as P

OFFSETS = (-2, -1, 1, 2)
STRAIN_EPS = 0.01
LOW_SPAN = 64


def shifted(value, axis, steps):
    count = lax.axis_size(axis)
    first, last = (max(0, -steps), min(count, count - steps))
    return lax.ppermute(value, axis, [(source, source + steps) for source in range(first, last)])


def entering_2(value, axis, combine, identity):
    devices, place = (lax.axis_size(axis), lax.axis_index(axis))
    everything = jax.tree.map(lambda part: lax.all_gather(part, axis), value)
    start = jax.tree.map(
        lambda part, zero: jnp.broadcast_to(jnp.asarray(zero, part.dtype), part.shape),
        value,
        identity,
    )

    def hop(k, before):
        reached = k < place
        new = combine(before, jax.tree.map(lambda part: part[k], everything))
        return jax.tree.map(lambda a, b: jnp.where(reached, a, b), new, before)

    return lax.fori_loop(0, devices, hop, start)


def basis_table():
    gauss_point = 1.0 / math.sqrt(3.0)
    xi_signs = [-1.0, 1.0, 1.0, -1.0, -1.0, 1.0, 1.0, -1.0]
    eta_signs = [-1.0, -1.0, 1.0, 1.0, -1.0, -1.0, 1.0, 1.0]
    zeta_signs = [1.0, 1.0, 1.0, 1.0, -1.0, -1.0, -1.0, -1.0]
    shape_table = [[0.0] * 8 for row_index in range(24)]
    for point_index in range(8):
        xi_point = gauss_point if point_index & 1 else -gauss_point
        eta_point = gauss_point if point_index & 2 else -gauss_point
        zeta_point = gauss_point if point_index & 4 else -gauss_point
        for node_index in range(8):
            along_xi = 1.0 + xi_signs[node_index] * xi_point
            along_eta = 1.0 + eta_signs[node_index] * eta_point
            along_zeta = 1.0 + zeta_signs[node_index] * zeta_point
            shape_table[point_index][node_index] = (
                xi_signs[node_index] * along_eta * along_zeta / 8.0
            )
            shape_table[8 + point_index][node_index] = (
                eta_signs[node_index] * along_xi * along_zeta / 8.0
            )
            shape_table[16 + point_index][node_index] = (
                zeta_signs[node_index] * along_xi * along_eta / 8.0
            )
    return shape_table


def strain_of(grad_x, grad_y, grad_z, first_comp, second_comp):
    return (
        grad_x[first_comp],
        grad_y[second_comp],
        0.5 * (grad_y[first_comp] + grad_x[second_comp]),
        0.5 * grad_z[first_comp],
        0.5 * grad_z[second_comp],
    )


def pairing(left_strain, right_strain):
    return (
        left_strain[0] * right_strain[0]
        + left_strain[1] * right_strain[1]
        + 0.5 * (left_strain[0] * right_strain[1] + left_strain[1] * right_strain[0])
        + left_strain[2] * right_strain[2]
        + left_strain[3] * right_strain[3]
        + left_strain[4] * right_strain[4]
    )


def element_terms(nodal_values, stretch, shear_part, thickness, rate_factor):
    layer_count = nodal_values.shape[1] - 1
    width = nodal_values.shape[3]
    top_nodes = nodal_values[:, :-1]
    bottom_nodes = nodal_values[:, 1:]
    hexa_nodes = jnp.concatenate([top_nodes, bottom_nodes], axis=2)
    basis = jnp.asarray(basis_table(), dtype=jnp.float32)
    derived = jnp.einsum("rn,clnb->clrb", basis, hexa_nodes, precision=lax.Precision.HIGHEST)
    derived = derived.reshape(4, layer_count, 3, 8, width)
    along_xi = derived[:, :, 0]
    along_eta = derived[:, :, 1]
    along_zeta = derived[:, :, 2]
    grad_x = stretch[0] * along_xi + shear_part[0] * along_eta
    grad_y = shear_part[1] * along_xi + stretch[1] * along_eta
    grad_z = (2.0 / thickness)[None, :, None, :] * along_zeta
    flow_strain = strain_of(grad_x, grad_y, grad_z, 0, 1)
    adjoint_strain = strain_of(grad_x, grad_y, grad_z, 2, 3)
    effective = pairing(flow_strain, flow_strain) + STRAIN_EPS
    viscosity = 0.5 * rate_factor[:, None, :] * jnp.power(effective, -1.0 / 3.0)
    volume = 0.5 * thickness / (stretch[0] * stretch[1] - shear_part[0] * shear_part[1])
    return volume * jnp.sum(4.0 * viscosity * pairing(flow_strain, adjoint_strain), axis=1)


def high_select(node_ids, high_count, dtype):
    high_part = node_ids // LOW_SPAN
    return (jnp.arange(high_count, dtype=jnp.int32)[:, None] == high_part[None, :]).astype(dtype)


def low_select(node_ids):
    low_part = node_ids % LOW_SPAN
    return (jnp.arange(LOW_SPAN, dtype=jnp.int32)[:, None] == low_part[None, :]).astype(jnp.float32)


def compose(earlier, later):
    return (earlier[0] * later[0], later[0] * earlier[1] + later[1])


def shards(
    velocity,
    adjoint,
    corners,
    shared,
    stretch,
    shear_part,
    thickness,
    rate_factor,
    retention,
    weight,
):
    owned_count = velocity.shape[2]
    layer_count = velocity.shape[1]
    slot_count = shared.shape[1]
    elem_count = corners.shape[1]
    fields = jnp.concatenate([velocity, adjoint], axis=0)
    padded = jnp.concatenate([fields, jnp.zeros((4, layer_count, 1), fields.dtype)], axis=2)
    outgoing = [jnp.take(padded, shared[direction], axis=2) for direction in range(4)]
    incoming = [
        shifted(outgoing[3 - direction], "plane", -OFFSETS[direction]) for direction in range(4)
    ]
    local_fields = jnp.concatenate([fields] + incoming, axis=2)
    local_count = local_fields.shape[2]
    high_count = local_count // LOW_SPAN
    below_level = shifted(local_fields[:, 0], "layer", -1)
    levels = jnp.concatenate([local_fields, below_level[:, None]], axis=1)
    level_rows = 4 * (layer_count + 1)
    level_table = levels.reshape(level_rows, high_count, LOW_SPAN)
    level_table = jnp.transpose(level_table, (0, 2, 1)).reshape(level_rows * LOW_SPAN, high_count)
    block_size = min(1024, elem_count)
    block_count = elem_count // block_size

    def one_block(block_start):
        corner_ids = lax.dynamic_slice_in_dim(corners, block_start, block_size, 1).reshape(-1)
        picked = jnp.dot(
            level_table,
            high_select(corner_ids, high_count, jnp.bfloat16),
            preferred_element_type=jnp.float32,
        )
        picked = picked.reshape(level_rows, LOW_SPAN, 4 * block_size)
        nodal_values = jnp.sum(picked * low_select(corner_ids)[None], axis=1)
        nodal_values = nodal_values.reshape(4, layer_count + 1, 4, block_size)
        return element_terms(
            nodal_values,
            lax.dynamic_slice_in_dim(stretch, block_start, block_size, 1),
            lax.dynamic_slice_in_dim(shear_part, block_start, block_size, 1),
            lax.dynamic_slice_in_dim(thickness, block_start, block_size, 1),
            lax.dynamic_slice_in_dim(rate_factor, block_start, block_size, 1),
        )

    layer_terms = lax.map(one_block, jnp.arange(block_count, dtype=jnp.int32) * block_size)
    layer_terms = jnp.transpose(layer_terms, (1, 0, 2)).reshape(layer_count, elem_count)
    factor = jnp.ones((elem_count,), jnp.float32)
    offset = jnp.zeros((elem_count,), jnp.float32)
    for layer_index in range(layer_count):
        factor = retention[layer_index] * factor
        offset = (
            retention[layer_index] * offset + (1.0 - retention[layer_index]) * weight[layer_index]
        )
    identity = (jnp.ones((elem_count,), jnp.float32), jnp.zeros((elem_count,), jnp.float32))
    _, entering = entering_2((factor, offset), "layer", compose, identity)
    running = entering
    column = jnp.zeros((elem_count,), jnp.float32)
    for layer_index in range(layer_count):
        running = (
            retention[layer_index] * running + (1.0 - retention[layer_index]) * weight[layer_index]
        )
        column = column + running * layer_terms[layer_index]
    quarter = 0.25 * column

    def add_block(block_index, node_table):
        block_start = block_index * block_size
        corner_ids = lax.dynamic_slice_in_dim(corners, block_start, block_size, 1).reshape(-1)
        values = jnp.tile(lax.dynamic_slice_in_dim(quarter, block_start, block_size, 0), 4)
        low_values = low_select(corner_ids) * values[None, :]
        return node_table + jnp.dot(
            low_values,
            high_select(corner_ids, high_count, jnp.float32).T,
            precision=lax.Precision.HIGHEST,
            preferred_element_type=jnp.float32,
        )

    node_table = lax.fori_loop(
        0, block_count, add_block, jnp.zeros((LOW_SPAN, high_count), jnp.float32)
    )
    partial_nodes = jnp.transpose(node_table).reshape(local_count)
    summed = lax.psum(partial_nodes, "layer")
    ghost_part = summed[owned_count:].reshape(4, slot_count)
    arriving = [
        shifted(ghost_part[3 - direction], "plane", -OFFSETS[direction]) for direction in range(4)
    ]
    owned_sum = jnp.concatenate([summed[:owned_count], jnp.zeros((1,), jnp.float32)])
    for direction in range(4):
        owned_sum = owned_sum.at[shared[direction]].add(arriving[direction])
    return owned_sum[:owned_count]


def solution(mesh):
    return jax.shard_map(
        shards,
        mesh=mesh,
        in_specs=(
            P(None, "layer", "plane"),
            P(None, "layer", "plane"),
            P(None, "plane"),
            P(None, "plane"),
            P(None, "plane"),
            P(None, "plane"),
            P("layer", "plane"),
            P("layer", "plane"),
            P("layer", "plane"),
            P("layer", "plane"),
        ),
        out_specs=P("plane"),
        check_vma=False,
    )
```

profile of v0, /device:TPU:2, one launch (start us, length us, event | category | flops | bytes accessed | tf_op | source)
XLA Modules:
  0.0 332.4 jit_solution(698319157925830426)
XLA Ops:
  1.9 4.6 %copy.48 = bf16[4,8,4096]{1,0,2:T(4,128)(2,1)} copy(bf16[4,8,4096]{2,1,0:T(8,128)(2,1)S(1)} %pad_maximum_fusion.1) | data formatting | bytes 524288 | tf_op jit(solution)/shard_map/concatenate | solution.py:135
  6.5 6.8 %concatenate.22 = bf16[4,8,4097]{1,0,2:T(4,128)(2,1)} pad(bf16[4,8,4096]{1,0,2:T(4,128)(2,1)} %copy.48, bf16[]{:T(256)} %constant.242.clone.1), padding=0_0x0_0x0_1 | pad | bytes 524354 | tf_op jit(solution)/shard_map/concatenate | solution.py:136
  16.5 4.5 %collective-permute-start = (bf16[4,8,128]{1,0,2:T(4,128)(2,1)S(1)}, bf16[4,8,128]{1,0,2:T(4,128)(2,1)S(1)}, u32[]{:S(2)}, u32[]{:S(2)}) collective-permute-start(bf16[4,8,128]{1,0,2:T(4,128)(2,1)S(1)} %select_bitcast_fusion.3), channel_id=1, source_target_pairs={{0,2},{1,3},{2,4},{3,5},{4,6},{5,7},{6,8},{7,9},{8,10},{9,11},{10,... | collective-permute-start | bytes 24584 | tf_op jit(solution)/shard_map/ppermute | solution.py:15
  24.2 3.5 %collective-permute-start.1 = (bf16[4,8,128]{1,0,2:T(4,128)(2,1)S(1)}, bf16[4,8,128]{1,0,2:T(4,128)(2,1)S(1)}, u32[]{:S(2)}, u32[]{:S(2)}) collective-permute-start(bf16[4,8,128]{1,0,2:T(4,128)(2,1)S(1)} %select_bitcast_fusion.2), channel_id=1, source_target_pairs={{0,1},{1,2},{2,3},{3,4},{4,5},{5,6},{6,7},{7,8},{8,9},{9,10},{10,1... | collective-permute-start | bytes 24584 | tf_op jit(solution)/shard_map/ppermute | solution.py:15
  30.8 4.5 %collective-permute-start.2 = (bf16[4,8,128]{1,0,2:T(4,128)(2,1)S(1)}, bf16[4,8,128]{1,0,2:T(4,128)(2,1)S(1)}, u32[]{:S(2)}, u32[]{:S(2)}) collective-permute-start(bf16[4,8,128]{1,0,2:T(4,128)(2,1)S(1)} %select_bitcast_fusion.1), channel_id=1, source_target_pairs={{1,0},{2,1},{3,2},{4,3},{5,4},{6,5},{7,6},{8,7},{9,8},{10,9},{11,1... | collective-permute-start | bytes 24584 | tf_op jit(solution)/shard_map/ppermute | solution.py:15
  43.3 23.9 %all-gather = f32[16,1,4096]{2,1,0:T(1,128)S(1)} all-gather(f32[1,1,4096]{2,1,0:T(1,128)S(1)} %get-tuple-element.500), channel_id=1, replica_groups=mesh['layer'=16,'plane'=32] {'layer'}, dimensions={0}, use_global_device_ids=true | all-gather | bytes 278528 | tf_op jit(solution)/shard_map/all_gather | solution.py:20
  67.3 15.2 %all-gather.1 = f32[16,1,4096]{2,1,0:T(1,128)S(1)} all-gather(f32[1,1,4096]{2,1,0:T(1,128)S(1)} %get-tuple-element.496), channel_id=1, replica_groups=mesh['layer'=16,'plane'=32] {'layer'}, dimensions={0}, use_global_device_ids=true | all-gather | bytes 278528 | tf_op jit(solution)/shard_map/all_gather | solution.py:20
  89.8 163.1 %while.43 = (s32[]{:T(128)}, f32[4,8,1024]{2,1,0:T(8,128)S(1)}, s32[4]{0:T(128)S(1)}, f32[8,4096]{1,0:T(8,128)S(1)}, f32[2,4096]{1,0:T(2,128)}, /*index=5*/f32[2...) while((s32[]{:T(128)}, f32[4,8,1024]{2,1,0:T(8,128)S(1)}, ...), condition=%wide.region_5.7_spmd.clone, body=%wide.region_2.6_spmd.sunk.clone.sunk | while | flops 1458830336 | bytes 95925216 | solution.py:170
  92.4 16.0 %fusion.57 = f32[4096,2304]{0,1:T(8,128)} fusion(bf16[2304,72]{1,0:T(8,128)(2,1)} %get-tuple-element.719, s32[4096]{0:T(1024)S(1)} %get-tuple-element.656), kind=kOutput, calls=%fused_computation.11.clone.1 | convolution fusion | flops 1359249408 | bytes 38096896 | tf_op jit(solution)/shard_map/while/body/eval_jaxpr/dot_general | solution.py:154
  108.5 14.8 %multiply_reduce_fusion.2 = f32[36,4096]{1,0:T(8,128)S(1)} fusion(f32[36,64,4096]{2,1,0:T(8,128)} %bitcast.239, f32[64,4096]{1,0:T(8,128)S(1)} %fusion.58), kind=kLoop, calls=%fused_computation.8.clone.1 | loop fusion | flops 18726912 | bytes 39387136 | tf_op jit(solution)/shard_map/while/body/eval_jaxpr/reduce_sum | solution.py:160
  124.0 3.6 %convolution_bitcast_fusion.2 = f32[4,8,3,8,1024]{4,3,2,1,0:T(8,128)S(1)} fusion(f32[24,8,1,1]{0,1,3,2:T(8,128)S(1)} %get-tuple-element.721, f32[4,8,4,1024]{3,2,1,0:T(4,128)S(1)} %get-tuple-element.658, f32[4,8,4,1024]{3,2,1,0:T(4,128)S(1)} %get-tuple-element.659), kind=kOutput, calls=%fused_computation.9.clone.1 | convolution fusion | flops 75759616 | bytes 4195072 | tf_op jit(solution)/shard_map/while/body/eval_jaxpr/rn,clnb->clrb/dot_general | solution.py:89
  133.2 16.0 %fusion.57 = f32[4096,2304]{0,1:T(8,128)} fusion(bf16[2304,72]{1,0:T(8,128)(2,1)} %get-tuple-element.719, s32[4096]{0:T(1024)S(1)} %get-tuple-element.656), kind=kOutput, calls=%fused_computation.11.clone.1 | convolution fusion | flops 1359249408 | bytes 38096896 | tf_op jit(solution)/shard_map/while/body/eval_jaxpr/dot_general | solution.py:154
  149.3 14.8 %multiply_reduce_fusion.2 = f32[36,4096]{1,0:T(8,128)S(1)} fusion(f32[36,64,4096]{2,1,0:T(8,128)} %bitcast.239, f32[64,4096]{1,0:T(8,128)S(1)} %fusion.58), kind=kLoop, calls=%fused_computation.8.clone.1 | loop fusion | flops 18726912 | bytes 39387136 | tf_op jit(solution)/shard_map/while/body/eval_jaxpr/reduce_sum | solution.py:160
  164.7 3.6 %convolution_bitcast_fusion.2 = f32[4,8,3,8,1024]{4,3,2,1,0:T(8,128)S(1)} fusion(f32[24,8,1,1]{0,1,3,2:T(8,128)S(1)} %get-tuple-element.721, f32[4,8,4,1024]{3,2,1,0:T(4,128)S(1)} %get-tuple-element.658, f32[4,8,4,1024]{3,2,1,0:T(4,128)S(1)} %get-tuple-element.659), kind=kOutput, calls=%fused_computation.9.clone.1 | convolution fusion | flops 75759616 | bytes 4195072 | tf_op jit(solution)/shard_map/while/body/eval_jaxpr/rn,clnb->clrb/dot_general | solution.py:89
  174.0 16.0 %fusion.57 = f32[4096,2304]{0,1:T(8,128)} fusion(bf16[2304,72]{1,0:T(8,128)(2,1)} %get-tuple-element.719, s32[4096]{0:T(1024)S(1)} %get-tuple-element.656), kind=kOutput, calls=%fused_computation.11.clone.1 | convolution fusion | flops 1359249408 | bytes 38096896 | tf_op jit(solution)/shard_map/while/body/eval_jaxpr/dot_general | solution.py:154
  190.1 14.8 %multiply_reduce_fusion.2 = f32[36,4096]{1,0:T(8,128)S(1)} fusion(f32[36,64,4096]{2,1,0:T(8,128)} %bitcast.239, f32[64,4096]{1,0:T(8,128)S(1)} %fusion.58), kind=kLoop, calls=%fused_computation.8.clone.1 | loop fusion | flops 18726912 | bytes 39387136 | tf_op jit(solution)/shard_map/while/body/eval_jaxpr/reduce_sum | solution.py:160
  205.5 3.6 %convolution_bitcast_fusion.2 = f32[4,8,3,8,1024]{4,3,2,1,0:T(8,128)S(1)} fusion(f32[24,8,1,1]{0,1,3,2:T(8,128)S(1)} %get-tuple-element.721, f32[4,8,4,1024]{3,2,1,0:T(4,128)S(1)} %get-tuple-element.658, f32[4,8,4,1024]{3,2,1,0:T(4,128)S(1)} %get-tuple-element.659), kind=kOutput, calls=%fused_computation.9.clone.1 | convolution fusion | flops 75759616 | bytes 4195072 | tf_op jit(solution)/shard_map/while/body/eval_jaxpr/rn,clnb->clrb/dot_general | solution.py:89
  214.8 16.0 %fusion.57 = f32[4096,2304]{0,1:T(8,128)} fusion(bf16[2304,72]{1,0:T(8,128)(2,1)} %get-tuple-element.719, s32[4096]{0:T(1024)S(1)} %get-tuple-element.656), kind=kOutput, calls=%fused_computation.11.clone.1 | convolution fusion | flops 1359249408 | bytes 38096896 | tf_op jit(solution)/shard_map/while/body/eval_jaxpr/dot_general | solution.py:154
  230.9 14.8 %multiply_reduce_fusion.2 = f32[36,4096]{1,0:T(8,128)S(1)} fusion(f32[36,64,4096]{2,1,0:T(8,128)} %bitcast.239, f32[64,4096]{1,0:T(8,128)S(1)} %fusion.58), kind=kLoop, calls=%fused_computation.8.clone.1 | loop fusion | flops 18726912 | bytes 39387136 | tf_op jit(solution)/shard_map/while/body/eval_jaxpr/reduce_sum | solution.py:160
  246.3 3.6 %convolution_bitcast_fusion.2 = f32[4,8,3,8,1024]{4,3,2,1,0:T(8,128)S(1)} fusion(f32[24,8,1,1]{0,1,3,2:T(8,128)S(1)} %get-tuple-element.721, f32[4,8,4,1024]{3,2,1,0:T(4,128)S(1)} %get-tuple-element.658, f32[4,8,4,1024]{3,2,1,0:T(4,128)S(1)} %get-tuple-element.659), kind=kOutput, calls=%fused_computation.9.clone.1 | convolution fusion | flops 75759616 | bytes 4195072 | tf_op jit(solution)/shard_map/while/body/eval_jaxpr/rn,clnb->clrb/dot_general | solution.py:89
  254.1 8.7 %while.45 = (s32[]{:T(128)}, f32[64,72]{1,0:T(8,128)}, s32[4,4096]{1,0:T(4,128)S(1)}, f32[4096]{0:T(1024)S(1)}, s32[]{:T(128)}, /*index=5*/s32[]{:T(128)}, s32[]{:T(128)}, s32[]{:T(128)}) while((s32[]{:T(128)}, f32[64,72]{1,0:T(8,128)}, s32[4,4096]{1,0:T(4,128)S(1)}, f32[4096]{0:T(1024)S(1)}, s32[]{:T(128)}, /*index=5*/s32[]{:T(128)}, ...), condition=%wide.region_7.9_spmd.clone, body=%wide.region_6.8_spmd.clone.sunk | while | flops 227398656 | bytes 229525 | solution.py:202
  263.7 48.1 %psum.7 = f32[4608]{0:T(1024)S(1)} all-reduce(f32[4608]{0:T(1024)S(1)} %reshape.352), channel_id=1, replica_groups=mesh['layer'=16,'plane'=32] {'layer'}, use_global_device_ids=true, to_apply=%region_8.10 | all-reduce | flops 4608 | bytes 36864 | tf_op jit(solution)/shard_map/psum | solution.py:206
  311.7 4.5 %collective-permute-start.5 = (f32[128]{0:T(128)S(1)}, f32[128]{0:T(128)S(1)}, u32[]{:S(2)}, u32[]{:S(2)}) collective-permute-start(f32[128]{0:T(128)S(1)} %get-tuple-element.525), channel_id=1, source_target_pairs={{0,2},{1,3},{2,4},{3,5},{4,6},{5,7},{6,8},{7,9},{8,10},{9,11},{10,... | collective-permute-start | bytes 1544 | tf_op jit(solution)/shard_map/ppermute | solution.py:15
  318.4 5.8 %collective-permute-start.7 = (f32[128]{0:T(128)S(1)}, f32[128]{0:T(128)S(1)}, u32[]{:S(2)}, u32[]{:S(2)}) collective-permute-start(f32[128]{0:T(128)S(1)} %get-tuple-element.523), channel_id=1, source_target_pairs={{1,0},{2,1},{3,2},{4,3},{5,4},{6,5},{7,6},{8,7},{9,8},{10,9},{11,1... | collective-permute-start | bytes 1544 | tf_op jit(solution)/shard_map/ppermute | solution.py:15
  (200 shorter events, 65.5 us)
Async XLA Ops:
  6.5 34.5 %copy-start.3 = (f32[8,4096]{1,0:T(8,128)S(1)}, f32[8,4096]{1,0:T(8,128)}, u32[]{:S(2)}) copy-start(f32[8,4096]{1,0:T(8,128)} %param.27) | copy-start | bytes 393220
  6.5 35.2 %copy-start.4 = (f32[8,4096]{1,0:T(8,128)S(1)}, f32[8,4096]{1,0:T(8,128)}, u32[]{:S(2)}) copy-start(f32[8,4096]{1,0:T(8,128)} %param.28) | copy-start | bytes 393220
  6.5 36.8 %copy-start.6 = (bf16[2,8,4096]{2,1,0:T(8,128)(2,1)S(1)}, bf16[2,8,4096]{2,1,0:T(8,128)(2,1)}, u32[]{:S(2)}) copy-start(bf16[2,8,4096]{2,1,0:T(8,128)(2,1)} %param.20) | copy-start | bytes 393220
  13.3 70.6 %copy-start.12 = (s32[4,128]{1,0:T(4,128)S(1)}, s32[4,128]{1,0:T(4,128)}, u32[]{:S(2)}) copy-start(s32[4,128]{1,0:T(4,128)} %param.22) | copy-start | bytes 6148
  16.5 68.0 %collective-permute-start = (bf16[4,8,128]{1,0,2:T(4,128)(2,1)S(1)}, bf16[4,8,128]{1,0,2:T(4,128)(2,1)S(1)}, u32[]{:S(2)}, u32[]{:S(2)}) collective-permute-start(bf16[4,8,128]{1,0,2:T(4,128)(2,1)S(1)} %select_bitcast_fusion.3), channel_id=1, source_target_pairs={{0,2},{1,3},{2,4},{3,5},{4,6},{5,7},{6,8},{7,9},{8,10},{9,11},{10,... | collective-permute-start | bytes 24584 | tf_op jit(solution)/shard_map/ppermute | solution.py:15
  24.2 60.4 %collective-permute-start.1 = (bf16[4,8,128]{1,0,2:T(4,128)(2,1)S(1)}, bf16[4,8,128]{1,0,2:T(4,128)(2,1)S(1)}, u32[]{:S(2)}, u32[]{:S(2)}) collective-permute-start(bf16[4,8,128]{1,0,2:T(4,128)(2,1)S(1)} %select_bitcast_fusion.2), channel_id=1, source_target_pairs={{0,1},{1,2},{2,3},{3,4},{4,5},{5,6},{6,7},{7,8},{8,9},{9,10},{10,1... | collective-permute-start | bytes 24584 | tf_op jit(solution)/shard_map/ppermute | solution.py:15
  30.8 53.9 %collective-permute-start.2 = (bf16[4,8,128]{1,0,2:T(4,128)(2,1)S(1)}, bf16[4,8,128]{1,0,2:T(4,128)(2,1)S(1)}, u32[]{:S(2)}, u32[]{:S(2)}) collective-permute-start(bf16[4,8,128]{1,0,2:T(4,128)(2,1)S(1)} %select_bitcast_fusion.1), channel_id=1, source_target_pairs={{1,0},{2,1},{3,2},{4,3},{5,4},{6,5},{7,6},{8,7},{9,8},{10,9},{11,1... | collective-permute-start | bytes 24584 | tf_op jit(solution)/shard_map/ppermute | solution.py:15
  38.5 51.3 %copy-start = (f32[8,4096]{1,0:T(8,128)S(1)}, f32[8,4096]{1,0:T(8,128)}, u32[]{:S(2)}) copy-start(f32[8,4096]{1,0:T(8,128)} %param.25) | copy-start | bytes 393220
  38.5 51.3 %copy-start.7 = (s32[4,4096]{1,0:T(4,128)S(1)}, s32[4,4096]{1,0:T(4,128)}, u32[]{:S(2)}) copy-start(s32[4,4096]{1,0:T(4,128)} %param.21) | copy-start | bytes 196612
  38.5 51.3 %copy-start.8 = (f32[24,8,1,1]{0,1,3,2:T(8,128)S(1)}, f32[24,8,1,1]{0,1,3,2:T(8,128)}, u32[]{:S(2)}) copy-start(f32[24,8,1,1]{0,1,3,2:T(8,128)} %constant.375) | copy-start | bytes 2308
  38.5 46.3 %collective-permute-start.3 = (bf16[4,8,128]{1,0,2:T(4,128)(2,1)S(1)}, bf16[4,8,128]{1,0,2:T(4,128)(2,1)S(1)}, u32[]{:S(2)}, u32[]{:S(2)}) collective-permute-start(bf16[4,8,128]{1,0,2:T(4,128)(2,1)S(1)} %select_bitcast_fusion), channel_id=1, source_target_pairs={{2,0},{3,1},{4,2},{5,3},{6,4},{7,5},{8,6},{9,7},{10,8},{11,9},{12,... | collective-permute-start | bytes 24584 | tf_op jit(solution)/shard_map/ppermute | solution.py:15
  85.0 3.1 collective-permute-start.4
  89.8 163.3 %copy-start.2 = (f32[4096]{0:T(1024)S(1)}, f32[4096]{0:T(1024)}, u32[]{:S(2)}) copy-start(f32[4096]{0:T(1024)} %copy-done.1) | copy-start | bytes 49156
  89.8 163.3 %copy-start.9 = (f32[1,4096]{1,0:T(1,128)S(1)}, f32[1,4096]{1,0:T(1,128)}, u32[]{:S(2)}) copy-start(f32[1,4096]{1,0:T(1,128)} %get-tuple-element.501) | copy-start | bytes 49156
  89.8 163.3 %copy-start.10 = (f32[1,4096]{1,0:T(1,128)S(1)}, f32[1,4096]{1,0:T(1,128)}, u32[]{:S(2)}) copy-start(f32[1,4096]{1,0:T(1,128)} %get-tuple-element.502) | copy-start | bytes 49156
  89.8 163.3 %copy-start.11 = (f32[1,4096]{1,0:T(1,128)S(1)}, f32[1,4096]{1,0:T(1,128)}, u32[]{:S(2)}) copy-start(f32[1,4096]{1,0:T(1,128)} %get-tuple-element.503) | copy-start | bytes 49156
  252.9 73.5 %copy-start.16 = (s32[128]{0:T(128)S(1)}, s32[128]{0:T(128)}, u32[]{:S(2)}) copy-start(s32[128]{0:T(128)} %get-tuple-element.529) | copy-start | bytes 1540
  254.0 73.8 %copy-start.15 = (s32[128]{0:T(128)S(1)}, s32[128]{0:T(128)}, u32[]{:S(2)}) copy-start(s32[128]{0:T(128)} %get-tuple-element.528) | copy-start | bytes 1540
  254.0 75.1 %copy-start.14 = (s32[128]{0:T(128)S(1)}, s32[128]{0:T(128)}, u32[]{:S(2)}) copy-start(s32[128]{0:T(128)} %get-tuple-element.527) | copy-start | bytes 1540
  254.0 76.5 %copy-start.13 = (s32[128]{0:T(128)S(1)}, s32[128]{0:T(128)}, u32[]{:S(2)}) copy-start(s32[128]{0:T(128)} %get-tuple-element.526) | copy-start | bytes 1540
  311.7 14.7 %collective-permute-start.5 = (f32[128]{0:T(128)S(1)}, f32[128]{0:T(128)S(1)}, u32[]{:S(2)}, u32[]{:S(2)}) collective-permute-start(f32[128]{0:T(128)S(1)} %get-tuple-element.525), channel_id=1, source_target_pairs={{0,2},{1,3},{2,4},{3,5},{4,6},{5,7},{6,8},{7,9},{8,10},{9,11},{10,... | collective-permute-start | bytes 1544 | tf_op jit(solution)/shard_map/ppermute | solution.py:15
  316.2 11.5 %collective-permute-start.6 = (f32[128]{0:T(128)S(1)}, f32[128]{0:T(128)S(1)}, u32[]{:S(2)}, u32[]{:S(2)}) collective-permute-start(f32[128]{0:T(128)S(1)} %get-tuple-element.524), channel_id=1, source_target_pairs={{0,1},{1,2},{2,3},{3,4},{4,5},{5,6},{6,7},{7,8},{8,9},{9,10},{10,1... | collective-permute-start | bytes 1544 | tf_op jit(solution)/shard_map/ppermute | solution.py:15
  318.4 10.7 %collective-permute-start.7 = (f32[128]{0:T(128)S(1)}, f32[128]{0:T(128)S(1)}, u32[]{:S(2)}, u32[]{:S(2)}) collective-permute-start(f32[128]{0:T(128)S(1)} %get-tuple-element.523), channel_id=1, source_target_pairs={{1,0},{2,1},{3,2},{4,3},{5,4},{6,5},{7,6},{8,7},{9,8},{10,9},{11,1... | collective-permute-start | bytes 1544 | tf_op jit(solution)/shard_map/ppermute | solution.py:15
  324.2 6.3 %collective-permute-start.8 = (f32[128]{0:T(128)S(1)}, f32[128]{0:T(128)S(1)}, u32[]{:S(2)}, u32[]{:S(2)}) collective-permute-start(f32[128]{0:T(128)S(1)} %get-tuple-element.522), channel_id=1, source_target_pairs={{2,0},{3,1},{4,2},{5,3},{6,4},{7,5},{8,6},{9,7},{10,8},{11,9},{12,... | collective-permute-start | bytes 1544 | tf_op jit(solution)/shard_map/ppermute | solution.py:15
  (2 other events, 38.8 us)
where the time goes:
time: 335 us; the launch traced here: 332 us
  blocking collectives  87.1 us (26%)
  matrix products  86.8 us (26%)
  other arithmetic  82.7 us (25%)
  local copies, waits for them, and re-layouts  33.9 us (10%)
  starting transfers between devices  31 us (9%)
  loops' own time  8.69 us (3%)
    dot_general x4, matrix products, one_block(): jnp.dot(level_table, high_select(corner_ids, high_count, jnp.bfloat16), p...  63.9 us
    reduce_sum x4, other arithmetic, one_block(): nodal_values = jnp.sum(picked * low_select(corner_ids)[None], axis=1)  59.2 us
    psum x1, blocking collectives, shards(): summed = lax.psum(partial_nodes, 'layer')  48.1 us
    all_gather x2, blocking collectives, entering_2(): everything = jax.tree.map(lambda part: lax.all_gather(part, axis), value)  39 us
    ppermute x9, starting transfers between devices, shifted(): lax.ppermute(value, axis, [(source, source + steps) for source in range(f...  31 us
    dot_general x4, matrix products, element_terms(): jnp.einsum('rn,clnb->clrb', basis, hexa_nodes, precision=lax.Precision.HI...  14.5 us
    gather x4, local copies, waits for them, and re-layouts, shards(): jnp.take(padded, shared[direction], axis=2)  11.8 us
    dot_general x4, matrix products, add_block(): jnp.dot(low_values, high_select(corner_ids, high_count, jnp.float32).T, p...  8.37 us
  transfers between devices with their start and end apart: 9, of which 2 were waited for; matrix products, arithmetic and copies ran while one was open for 5% of the time, Pallas kernels for 0%

commit v1 on v0

--- a/solution.py
+++ b/solution.py
@@ -203,7 +203,7 @@
         0, block_count, add_block, jnp.zeros((LOW_SPAN, high_count), jnp.float32)
     )
     partial_nodes = jnp.transpose(node_table).reshape(local_count)
-    summed = lax.psum(partial_nodes, "layer")
+    summed = jnp.sum(lax.all_gather(partial_nodes, "layer"), axis=0)
     ghost_part = summed[owned_count:].reshape(4, slot_count)
     arriving = [
         shifted(ghost_part[3 - direction], "plane", -OFFSETS[direction]) for direction in range(4)

time: 335 us -> 304 us (0.907)
  blocking collectives: 87.1 us -> 56.5 us
    psum x1 -> x0, blocking collectives: 48.1 us -> none  [shards(): summed = lax.psum(partial_nodes, 'layer')]
    all_gather x0 -> x1, blocking collectives: none -> 17.5 us  [shards(): summed = jnp.sum(lax.all_gather(partial_nodes, 'layer'), axis=0)]
  transfers between devices with their start and end apart: 9 -> 9, of which waited for: 2 -> 2; matrix products, arithmetic and copies ran while one was open for 5% -> 6% of each run, Pallas kernels for 0% -> 0%
where the time goes in v1:
time: 304 us; the launch traced here: 302 us
  matrix products  86.8 us (29%)
  other arithmetic  82.9 us (27%)
  blocking collectives  56.5 us (19%)
  local copies, waits for them, and re-layouts  33.9 us (11%)
  starting transfers between devices  31 us (10%)
  loops' own time  8.69 us (3%)
    dot_general x4, matrix products, one_block(): jnp.dot(level_table, high_select(corner_ids, high_count, jnp.bfloat16), p...  63.9 us
    reduce_sum x4, other arithmetic, one_block(): nodal_values = jnp.sum(picked * low_select(corner_ids)[None], axis=1)  59.2 us
    all_gather x2, blocking collectives, entering_2(): everything = jax.tree.map(lambda part: lax.all_gather(part, axis), value)  39 us
    ppermute x9, starting transfers between devices, shifted(): lax.ppermute(value, axis, [(source, source + steps) for source in range(f...  31 us
    all_gather x1, blocking collectives, shards(): summed = jnp.sum(lax.all_gather(partial_nodes, 'layer'), axis=0)  17.5 us
    dot_general x4, matrix products, element_terms(): jnp.einsum('rn,clnb->clrb', basis, hexa_nodes, precision=lax.Precision.HI...  14.5 us
    gather x4, local copies, waits for them, and re-layouts, shards(): jnp.take(padded, shared[direction], axis=2)  11.8 us
    dot_general x4, matrix products, add_block(): jnp.dot(low_values, high_select(corner_ids, high_count, jnp.float32).T, p...  8.37 us
  transfers between devices with their start and end apart: 9, of which 2 were waited for; matrix products, arithmetic and copies ran while one was open for 6% of the time, Pallas kernels for 0%

profile of v1, /device:TPU:2, one launch (start us, length us, event | category | flops | bytes accessed | tf_op | source)
XLA Modules:
  0.0 302.1 jit_solution(6682381268800975701)
XLA Ops:
  1.9 4.6 %copy.48 = bf16[4,8,4096]{1,0,2:T(4,128)(2,1)} copy(bf16[4,8,4096]{2,1,0:T(8,128)(2,1)S(1)} %pad_maximum_fusion.1) | data formatting | bytes 524288 | tf_op jit(solution)/shard_map/concatenate | solution.py:135
  6.5 6.8 %concatenate.22 = bf16[4,8,4097]{1,0,2:T(4,128)(2,1)} pad(bf16[4,8,4096]{1,0,2:T(4,128)(2,1)} %copy.48, bf16[]{:T(256)} %constant.243.clone.1), padding=0_0x0_0x0_1 | pad | bytes 524354 | tf_op jit(solution)/shard_map/concatenate | solution.py:136
  16.5 4.5 %collective-permute-start = (bf16[4,8,128]{1,0,2:T(4,128)(2,1)S(1)}, bf16[4,8,128]{1,0,2:T(4,128)(2,1)S(1)}, u32[]{:S(2)}, u32[]{:S(2)}) collective-permute-start(bf16[4,8,128]{1,0,2:T(4,128)(2,1)S(1)} %select_bitcast_fusion.3), channel_id=1, source_target_pairs={{0,2},{1,3},{2,4},{3,5},{4,6},{5,7},{6,8},{7,9},{8,10},{9,11},{10,... | collective-permute-start | bytes 24584 | tf_op jit(solution)/shard_map/ppermute | solution.py:15
  24.2 3.5 %collective-permute-start.1 = (bf16[4,8,128]{1,0,2:T(4,128)(2,1)S(1)}, bf16[4,8,128]{1,0,2:T(4,128)(2,1)S(1)}, u32[]{:S(2)}, u32[]{:S(2)}) collective-permute-start(bf16[4,8,128]{1,0,2:T(4,128)(2,1)S(1)} %select_bitcast_fusion.2), channel_id=1, source_target_pairs={{0,1},{1,2},{2,3},{3,4},{4,5},{5,6},{6,7},{7,8},{8,9},{9,10},{10,1... | collective-permute-start | bytes 24584 | tf_op jit(solution)/shard_map/ppermute | solution.py:15
  30.8 4.5 %collective-permute-start.2 = (bf16[4,8,128]{1,0,2:T(4,128)(2,1)S(1)}, bf16[4,8,128]{1,0,2:T(4,128)(2,1)S(1)}, u32[]{:S(2)}, u32[]{:S(2)}) collective-permute-start(bf16[4,8,128]{1,0,2:T(4,128)(2,1)S(1)} %select_bitcast_fusion.1), channel_id=1, source_target_pairs={{1,0},{2,1},{3,2},{4,3},{5,4},{6,5},{7,6},{8,7},{9,8},{10,9},{11,1... | collective-permute-start | bytes 24584 | tf_op jit(solution)/shard_map/ppermute | solution.py:15
  43.3 23.9 %all-gather = f32[16,1,4096]{2,1,0:T(1,128)S(1)} all-gather(f32[1,1,4096]{2,1,0:T(1,128)S(1)} %get-tuple-element.500), channel_id=1, replica_groups=mesh['layer'=16,'plane'=32] {'layer'}, dimensions={0}, use_global_device_ids=true | all-gather | bytes 278528 | tf_op jit(solution)/shard_map/all_gather | solution.py:20
  67.3 15.2 %all-gather.1 = f32[16,1,4096]{2,1,0:T(1,128)S(1)} all-gather(f32[1,1,4096]{2,1,0:T(1,128)S(1)} %get-tuple-element.496), channel_id=1, replica_groups=mesh['layer'=16,'plane'=32] {'layer'}, dimensions={0}, use_global_device_ids=true | all-gather | bytes 278528 | tf_op jit(solution)/shard_map/all_gather | solution.py:20
  89.8 163.1 %while.43 = (s32[]{:T(128)}, f32[4,8,1024]{2,1,0:T(8,128)S(1)}, s32[4]{0:T(128)S(1)}, f32[8,4096]{1,0:T(8,128)S(1)}, f32[2,4096]{1,0:T(2,128)}, /*index=5*/f32[2...) while((s32[]{:T(128)}, f32[4,8,1024]{2,1,0:T(8,128)S(1)}, ...), condition=%wide.region_5.7_spmd.clone, body=%wide.region_2.6_spmd.sunk.clone.sunk | while | flops 1458830336 | bytes 95925216 | solution.py:170
  92.4 16.0 %fusion.57 = f32[4096,2304]{0,1:T(8,128)} fusion(bf16[2304,72]{1,0:T(8,128)(2,1)} %get-tuple-element.719, s32[4096]{0:T(1024)S(1)} %get-tuple-element.656), kind=kOutput, calls=%fused_computation.11.clone.1 | convolution fusion | flops 1359249408 | bytes 38096896 | tf_op jit(solution)/shard_map/while/body/eval_jaxpr/dot_general | solution.py:154
  108.5 14.8 %multiply_reduce_fusion.2 = f32[36,4096]{1,0:T(8,128)S(1)} fusion(f32[36,64,4096]{2,1,0:T(8,128)} %bitcast.239, f32[64,4096]{1,0:T(8,128)S(1)} %fusion.58), kind=kLoop, calls=%fused_computation.8.clone.1 | loop fusion | flops 18726912 | bytes 39387136 | tf_op jit(solution)/shard_map/while/body/eval_jaxpr/reduce_sum | solution.py:160
  124.0 3.6 %convolution_bitcast_fusion.2 = f32[4,8,3,8,1024]{4,3,2,1,0:T(8,128)S(1)} fusion(f32[24,8,1,1]{0,1,3,2:T(8,128)S(1)} %get-tuple-element.721, f32[4,8,4,1024]{3,2,1,0:T(4,128)S(1)} %get-tuple-element.658, f32[4,8,4,1024]{3,2,1,0:T(4,128)S(1)} %get-tuple-element.659), kind=kOutput, calls=%fused_computation.9.clone.1 | convolution fusion | flops 75759616 | bytes 4195072 | tf_op jit(solution)/shard_map/while/body/eval_jaxpr/rn,clnb->clrb/dot_general | solution.py:89
  133.2 16.0 %fusion.57 = f32[4096,2304]{0,1:T(8,128)} fusion(bf16[2304,72]{1,0:T(8,128)(2,1)} %get-tuple-element.719, s32[4096]{0:T(1024)S(1)} %get-tuple-element.656), kind=kOutput, calls=%fused_computation.11.clone.1 | convolution fusion | flops 1359249408 | bytes 38096896 | tf_op jit(solution)/shard_map/while/body/eval_jaxpr/dot_general | solution.py:154
  149.3 14.8 %multiply_reduce_fusion.2 = f32[36,4096]{1,0:T(8,128)S(1)} fusion(f32[36,64,4096]{2,1,0:T(8,128)} %bitcast.239, f32[64,4096]{1,0:T(8,128)S(1)} %fusion.58), kind=kLoop, calls=%fused_computation.8.clone.1 | loop fusion | flops 18726912 | bytes 39387136 | tf_op jit(solution)/shard_map/while/body/eval_jaxpr/reduce_sum | solution.py:160
  164.7 3.6 %convolution_bitcast_fusion.2 = f32[4,8,3,8,1024]{4,3,2,1,0:T(8,128)S(1)} fusion(f32[24,8,1,1]{0,1,3,2:T(8,128)S(1)} %get-tuple-element.721, f32[4,8,4,1024]{3,2,1,0:T(4,128)S(1)} %get-tuple-element.658, f32[4,8,4,1024]{3,2,1,0:T(4,128)S(1)} %get-tuple-element.659), kind=kOutput, calls=%fused_computation.9.clone.1 | convolution fusion | flops 75759616 | bytes 4195072 | tf_op jit(solution)/shard_map/while/body/eval_jaxpr/rn,clnb->clrb/dot_general | solution.py:89
  174.0 16.0 %fusion.57 = f32[4096,2304]{0,1:T(8,128)} fusion(bf16[2304,72]{1,0:T(8,128)(2,1)} %get-tuple-element.719, s32[4096]{0:T(1024)S(1)} %get-tuple-element.656), kind=kOutput, calls=%fused_computation.11.clone.1 | convolution fusion | flops 1359249408 | bytes 38096896 | tf_op jit(solution)/shard_map/while/body/eval_jaxpr/dot_general | solution.py:154
  190.1 14.8 %multiply_reduce_fusion.2 = f32[36,4096]{1,0:T(8,128)S(1)} fusion(f32[36,64,4096]{2,1,0:T(8,128)} %bitcast.239, f32[64,4096]{1,0:T(8,128)S(1)} %fusion.58), kind=kLoop, calls=%fused_computation.8.clone.1 | loop fusion | flops 18726912 | bytes 39387136 | tf_op jit(solution)/shard_map/while/body/eval_jaxpr/reduce_sum | solution.py:160
  205.5 3.6 %convolution_bitcast_fusion.2 = f32[4,8,3,8,1024]{4,3,2,1,0:T(8,128)S(1)} fusion(f32[24,8,1,1]{0,1,3,2:T(8,128)S(1)} %get-tuple-element.721, f32[4,8,4,1024]{3,2,1,0:T(4,128)S(1)} %get-tuple-element.658, f32[4,8,4,1024]{3,2,1,0:T(4,128)S(1)} %get-tuple-element.659), kind=kOutput, calls=%fused_computation.9.clone.1 | convolution fusion | flops 75759616 | bytes 4195072 | tf_op jit(solution)/shard_map/while/body/eval_jaxpr/rn,clnb->clrb/dot_general | solution.py:89
  214.8 16.0 %fusion.57 = f32[4096,2304]{0,1:T(8,128)} fusion(bf16[2304,72]{1,0:T(8,128)(2,1)} %get-tuple-element.719, s32[4096]{0:T(1024)S(1)} %get-tuple-element.656), kind=kOutput, calls=%fused_computation.11.clone.1 | convolution fusion | flops 1359249408 | bytes 38096896 | tf_op jit(solution)/shard_map/while/body/eval_jaxpr/dot_general | solution.py:154
  230.9 14.8 %multiply_reduce_fusion.2 = f32[36,4096]{1,0:T(8,128)S(1)} fusion(f32[36,64,4096]{2,1,0:T(8,128)} %bitcast.239, f32[64,4096]{1,0:T(8,128)S(1)} %fusion.58), kind=kLoop, calls=%fused_computation.8.clone.1 | loop fusion | flops 18726912 | bytes 39387136 | tf_op jit(solution)/shard_map/while/body/eval_jaxpr/reduce_sum | solution.py:160
  246.3 3.6 %convolution_bitcast_fusion.2 = f32[4,8,3,8,1024]{4,3,2,1,0:T(8,128)S(1)} fusion(f32[24,8,1,1]{0,1,3,2:T(8,128)S(1)} %get-tuple-element.721, f32[4,8,4,1024]{3,2,1,0:T(4,128)S(1)} %get-tuple-element.658, f32[4,8,4,1024]{3,2,1,0:T(4,128)S(1)} %get-tuple-element.659), kind=kOutput, calls=%fused_computation.9.clone.1 | convolution fusion | flops 75759616 | bytes 4195072 | tf_op jit(solution)/shard_map/while/body/eval_jaxpr/rn,clnb->clrb/dot_general | solution.py:89
  254.1 8.7 %while.45 = (s32[]{:T(128)}, f32[64,72]{1,0:T(8,128)}, s32[4,4096]{1,0:T(4,128)S(1)}, f32[4096]{0:T(1024)S(1)}, s32[]{:T(128)}, /*index=5*/s32[]{:T(128)}, s32[]{:T(128)}, s32[]{:T(128)}) while((s32[]{:T(128)}, f32[64,72]{1,0:T(8,128)}, s32[4,4096]{1,0:T(4,128)S(1)}, f32[4096]{0:T(1024)S(1)}, s32[]{:T(128)}, /*index=5*/s32[]{:T(128)}, ...), condition=%wide.region_7.9_spmd.clone, body=%wide.region_6.8_spmd.clone.sunk | while | flops 227398656 | bytes 229525 | solution.py:202
  263.7 17.5 %all-gather.2 = f32[16,1,4608]{2,1,0:T(1,128)S(1)} all-gather(f32[1,1,4608]{2,1,0:T(1,128)S(1)} %reshape.439), channel_id=1, replica_groups=mesh['layer'=16,'plane'=32] {'layer'}, dimensions={0}, use_global_device_ids=true | all-gather | bytes 313344 | tf_op jit(solution)/shard_map/all_gather | solution.py:206
  281.4 4.5 %collective-permute-start.5 = (f32[128]{0:T(128)S(1)}, f32[128]{0:T(128)S(1)}, u32[]{:S(2)}, u32[]{:S(2)}) collective-permute-start(f32[128]{0:T(128)S(1)} %get-tuple-element.525), channel_id=1, source_target_pairs={{0,2},{1,3},{2,4},{3,5},{4,6},{5,7},{6,8},{7,9},{8,10},{9,11},{10,... | collective-permute-start | bytes 1544 | tf_op jit(solution)/shard_map/ppermute | solution.py:15
  288.0 5.8 %collective-permute-start.7 = (f32[128]{0:T(128)S(1)}, f32[128]{0:T(128)S(1)}, u32[]{:S(2)}, u32[]{:S(2)}) collective-permute-start(f32[128]{0:T(128)S(1)} %get-tuple-element.523), channel_id=1, source_target_pairs={{1,0},{2,1},{3,2},{4,3},{5,4},{6,5},{7,6},{8,7},{9,8},{10,9},{11,1... | collective-permute-start | bytes 1544 | tf_op jit(solution)/shard_map/ppermute | solution.py:15
  (201 shorter events, 65.7 us)
Async XLA Ops:
  6.5 34.5 %copy-start.3 = (f32[8,4096]{1,0:T(8,128)S(1)}, f32[8,4096]{1,0:T(8,128)}, u32[]{:S(2)}) copy-start(f32[8,4096]{1,0:T(8,128)} %param.27) | copy-start | bytes 393220
  6.5 35.2 %copy-start.4 = (f32[8,4096]{1,0:T(8,128)S(1)}, f32[8,4096]{1,0:T(8,128)}, u32[]{:S(2)}) copy-start(f32[8,4096]{1,0:T(8,128)} %param.28) | copy-start | bytes 393220
  6.5 36.8 %copy-start.6 = (bf16[2,8,4096]{2,1,0:T(8,128)(2,1)S(1)}, bf16[2,8,4096]{2,1,0:T(8,128)(2,1)}, u32[]{:S(2)}) copy-start(bf16[2,8,4096]{2,1,0:T(8,128)(2,1)} %param.20) | copy-start | bytes 393220
  13.3 70.6 %copy-start.12 = (s32[4,128]{1,0:T(4,128)S(1)}, s32[4,128]{1,0:T(4,128)}, u32[]{:S(2)}) copy-start(s32[4,128]{1,0:T(4,128)} %param.22) | copy-start | bytes 6148
  16.5 68.0 %collective-permute-start = (bf16[4,8,128]{1,0,2:T(4,128)(2,1)S(1)}, bf16[4,8,128]{1,0,2:T(4,128)(2,1)S(1)}, u32[]{:S(2)}, u32[]{:S(2)}) collective-permute-start(bf16[4,8,128]{1,0,2:T(4,128)(2,1)S(1)} %select_bitcast_fusion.3), channel_id=1, source_target_pairs={{0,2},{1,3},{2,4},{3,5},{4,6},{5,7},{6,8},{7,9},{8,10},{9,11},{10,... | collective-permute-start | bytes 24584 | tf_op jit(solution)/shard_map/ppermute | solution.py:15
  24.2 60.4 %collective-permute-start.1 = (bf16[4,8,128]{1,0,2:T(4,128)(2,1)S(1)}, bf16[4,8,128]{1,0,2:T(4,128)(2,1)S(1)}, u32[]{:S(2)}, u32[]{:S(2)}) collective-permute-start(bf16[4,8,128]{1,0,2:T(4,128)(2,1)S(1)} %select_bitcast_fusion.2), channel_id=1, source_target_pairs={{0,1},{1,2},{2,3},{3,4},{4,5},{5,6},{6,7},{7,8},{8,9},{9,10},{10,1... | collective-permute-start | bytes 24584 | tf_op jit(solution)/shard_map/ppermute | solution.py:15
  30.8 53.9 %collective-permute-start.2 = (bf16[4,8,128]{1,0,2:T(4,128)(2,1)S(1)}, bf16[4,8,128]{1,0,2:T(4,128)(2,1)S(1)}, u32[]{:S(2)}, u32[]{:S(2)}) collective-permute-start(bf16[4,8,128]{1,0,2:T(4,128)(2,1)S(1)} %select_bitcast_fusion.1), channel_id=1, source_target_pairs={{1,0},{2,1},{3,2},{4,3},{5,4},{6,5},{7,6},{8,7},{9,8},{10,9},{11,1... | collective-permute-start | bytes 24584 | tf_op jit(solution)/shard_map/ppermute | solution.py:15
  38.5 51.3 %copy-start = (f32[8,4096]{1,0:T(8,128)S(1)}, f32[8,4096]{1,0:T(8,128)}, u32[]{:S(2)}) copy-start(f32[8,4096]{1,0:T(8,128)} %param.25) | copy-start | bytes 393220
  38.5 51.3 %copy-start.7 = (s32[4,4096]{1,0:T(4,128)S(1)}, s32[4,4096]{1,0:T(4,128)}, u32[]{:S(2)}) copy-start(s32[4,4096]{1,0:T(4,128)} %param.21) | copy-start | bytes 196612
  38.5 51.3 %copy-start.8 = (f32[24,8,1,1]{0,1,3,2:T(8,128)S(1)}, f32[24,8,1,1]{0,1,3,2:T(8,128)}, u32[]{:S(2)}) copy-start(f32[24,8,1,1]{0,1,3,2:T(8,128)} %constant.376) | copy-start | bytes 2308
  38.5 46.3 %collective-permute-start.3 = (bf16[4,8,128]{1,0,2:T(4,128)(2,1)S(1)}, bf16[4,8,128]{1,0,2:T(4,128)(2,1)S(1)}, u32[]{:S(2)}, u32[]{:S(2)}) collective-permute-start(bf16[4,8,128]{1,0,2:T(4,128)(2,1)S(1)} %select_bitcast_fusion), channel_id=1, source_target_pairs={{2,0},{3,1},{4,2},{5,3},{6,4},{7,5},{8,6},{9,7},{10,8},{11,9},{12,... | collective-permute-start | bytes 24584 | tf_op jit(solution)/shard_map/ppermute | solution.py:15
  85.0 3.1 %collective-permute-start.4 = (bf16[4,4608]{1,0:T(4,128)(2,1)S(1)}, bf16[4,4608]{1,0:T(4,128)(2,1)S(1)}, u32[]{:S(2)}, u32[]{:S(2)}) collective-permute-start(bf16[4,4608]{1,0:T(4,128)(2,1)S(1)} %bitcast.276), channel_id=1, source_target_pairs={{32,0},{64,32},{96,64},{128,96},{160,128},{192,160},{224,192},{256... | collective-permute-start | bytes 110600 | tf_op jit(solution)/shard_map/ppermute | solution.py:15
  89.8 163.3 %copy-start.2 = (f32[4096]{0:T(1024)S(1)}, f32[4096]{0:T(1024)}, u32[]{:S(2)}) copy-start(f32[4096]{0:T(1024)} %copy-done.1) | copy-start | bytes 49156
  89.8 163.3 %copy-start.9 = (f32[1,4096]{1,0:T(1,128)S(1)}, f32[1,4096]{1,0:T(1,128)}, u32[]{:S(2)}) copy-start(f32[1,4096]{1,0:T(1,128)} %get-tuple-element.501) | copy-start | bytes 49156
  89.8 163.3 %copy-start.10 = (f32[1,4096]{1,0:T(1,128)S(1)}, f32[1,4096]{1,0:T(1,128)}, u32[]{:S(2)}) copy-start(f32[1,4096]{1,0:T(1,128)} %get-tuple-element.502) | copy-start | bytes 49156
  89.8 163.3 %copy-start.11 = (f32[1,4096]{1,0:T(1,128)S(1)}, f32[1,4096]{1,0:T(1,128)}, u32[]{:S(2)}) copy-start(f32[1,4096]{1,0:T(1,128)} %get-tuple-element.503) | copy-start | bytes 49156
  254.0 42.1 %copy-start.16 = (s32[128]{0:T(128)S(1)}, s32[128]{0:T(128)}, u32[]{:S(2)}) copy-start(s32[128]{0:T(128)} %get-tuple-element.529) | copy-start | bytes 1540
  254.0 43.4 %copy-start.15 = (s32[128]{0:T(128)S(1)}, s32[128]{0:T(128)}, u32[]{:S(2)}) copy-start(s32[128]{0:T(128)} %get-tuple-element.528) | copy-start | bytes 1540
  254.0 44.7 %copy-start.14 = (s32[128]{0:T(128)S(1)}, s32[128]{0:T(128)}, u32[]{:S(2)}) copy-start(s32[128]{0:T(128)} %get-tuple-element.527) | copy-start | bytes 1540
  254.0 46.1 %copy-start.13 = (s32[128]{0:T(128)S(1)}, s32[128]{0:T(128)}, u32[]{:S(2)}) copy-start(s32[128]{0:T(128)} %get-tuple-element.526) | copy-start | bytes 1540
  281.4 14.7 %collective-permute-start.5 = (f32[128]{0:T(128)S(1)}, f32[128]{0:T(128)S(1)}, u32[]{:S(2)}, u32[]{:S(2)}) collective-permute-start(f32[128]{0:T(128)S(1)} %get-tuple-element.525), channel_id=1, source_target_pairs={{0,2},{1,3},{2,4},{3,5},{4,6},{5,7},{6,8},{7,9},{8,10},{9,11},{10,... | collective-permute-start | bytes 1544 | tf_op jit(solution)/shard_map/ppermute | solution.py:15
  285.9 11.5 %collective-permute-start.6 = (f32[128]{0:T(128)S(1)}, f32[128]{0:T(128)S(1)}, u32[]{:S(2)}, u32[]{:S(2)}) collective-permute-start(f32[128]{0:T(128)S(1)} %get-tuple-element.524), channel_id=1, source_target_pairs={{0,1},{1,2},{2,3},{3,4},{4,5},{5,6},{6,7},{7,8},{8,9},{9,10},{10,1... | collective-permute-start | bytes 1544 | tf_op jit(solution)/shard_map/ppermute | solution.py:15
  288.0 10.7 %collective-permute-start.7 = (f32[128]{0:T(128)S(1)}, f32[128]{0:T(128)S(1)}, u32[]{:S(2)}, u32[]{:S(2)}) collective-permute-start(f32[128]{0:T(128)S(1)} %get-tuple-element.523), channel_id=1, source_target_pairs={{1,0},{2,1},{3,2},{4,3},{5,4},{6,5},{7,6},{8,7},{9,8},{10,9},{11,1... | collective-permute-start | bytes 1544 | tf_op jit(solution)/shard_map/ppermute | solution.py:15
  293.9 6.3 %collective-permute-start.8 = (f32[128]{0:T(128)S(1)}, f32[128]{0:T(128)S(1)}, u32[]{:S(2)}, u32[]{:S(2)}) collective-permute-start(f32[128]{0:T(128)S(1)} %get-tuple-element.522), channel_id=1, source_target_pairs={{2,0},{3,1},{4,2},{5,3},{6,4},{7,5},{8,6},{9,7},{10,8},{11,9},{12,... | collective-permute-start | bytes 1544 | tf_op jit(solution)/shard_map/ppermute | solution.py:15
  (2 other events, 38.8 us)
